TPU v7x, 128 devices: a whole 4x4x4 slice. The times are simulated.
128 devices in a mesh: rows: 8 (over x, z_lo), cols: 16 (over z_hi, y, core).
Axes of the slice: x: 4, y: 4, z: 4 (z_hi: 2, z_lo: 2; z = z_hi * 2 + z_lo), core: 2. Of those that a mesh axis runs over, the one named last changes fastest.
Arguments:
- ancestor_inv: bfloat16 [16384, 16384], P('rows', 'cols'), may hold values from -0.0625 to 0.0625
- lfactor: bfloat16 [32, 256, 6, 256], P('cols'), may hold values from -0.8984375 to 0.8984375
- struct: int32 [6, 32], replicated, may hold values from 0 to 63, as said below
- validity: int32 [6, 32], replicated, may hold values from 0 to 1, as said below
- diag_inverse: float32 [6, 256, 256], replicated, may hold values from -6 to 6
Outputs:
- column_block: bfloat16 [16384, 1536], P(('rows', 'cols'))
- diagonal_block: float32 [6, 256, 256], replicated
Inputs may be any that keep to these rules, and one draw needn't show every extreme that they name: `struct`: within a supernode the 32 tile indices are distinct and increasing, and every list holds tiles 0 and 63. `validity`: every tile index of 0 to 63 is a valid entry of some supernode's list; some supernode has all 32 flags set.
All inputs are finite; a program needn't handle non-finite values.
Results may differ from a plain program's by a relative error of at most 0.001.
Values may be sent and summed in bfloat16 or wider, within the bound.
No kernel may reach another device: no remote copies, remote signals or barrier semaphores. Data moves between devices by JAX's collectives and lax.ppermute only.
A program may use at most 192 MiB of HBM per device.

v0:
```python
import jax
import jax.numpy as jnp
from jax import lax
from jax.experimental import pallas as pl
from jax.experimental.pallas import tpu as pltpu
from jax.sharding import Mesh, PartitionSpec as P


BF16 = jnp.bfloat16
F32 = jnp.float32
I16 = jnp.int16
NX, NL, NH, NY, NC = 4, 2, 2, 4, 2
XL = ("x", "l")
HY = ("h", "y")
CHIPS = XL + HY
CORE_SWAP = [(0, 1), (1, 0)]
UP = [(i, (i + 1) % NX) for i in range(NX)]
DOWN = [(i, (i - 1) % NX) for i in range(NX)]
LEVELS = 32000.0
LOWEST = -100.0
LANES = 128


def level_of(top):
    return jnp.maximum(jnp.ceil(jnp.log2(jnp.maximum(top, 1e-37)) + 0.01), LOWEST)


def code(values, level):
    return jnp.round(values * (jnp.exp2(-level) * LEVELS)).astype(jnp.int32).astype(I16)


def plain(coded):
    return coded.astype(jnp.int32).astype(F32)


def scale_of(level):
    return jnp.exp2(level) * (1.0 / LEVELS)


def pick_kernel(place, where, x_ref, window_ref, own_ref):
    members, window = window_ref.shape[:2]
    groups = own_ref.shape[0]
    chip, core = where[0], where[1]
    for k in range(members):

        def tile(t):
            p = place[core * members + k, t]
            block = x_ref[jnp.maximum(p, 0), k]
            return jnp.where(p >= 0, block, jnp.zeros_like(block))

        for s in range(window):
            window_ref[k, s] = tile(chip * window + s)
        for g in range(groups):
            own_ref[g, k] = tile(g * window + chip)


def product_kernel(place, where, own_ref, other_ref, *refs):
    inputs = NL * NX
    parts, outs = refs[:inputs], refs[inputs : inputs + NH * NY]
    panel, sems = refs[inputs + NH * NY :]
    members, window, _, _, size = panel.shape
    half = own_ref.shape[1] // size
    core, group, x, l, h, y = (where[i] for i in range(1, 7))
    step = pl.program_id(0)
    tile = group * window + lax.rem(h + step // NY, NH) * NY + lax.rem(y + step, NY)

    @pl.when(step == 0)
    def _():
        copies = []
        for side in range(NL):
            for hop, shift in enumerate(RING):
                source = lax.rem(x + shift, NX) * NL + lax.rem(l + side, NL)
                i = side * NX + hop
                copies.append(pltpu.make_async_copy(parts[i], panel.at[:, :, source], sems.at[i]))
        for copy in copies:
            copy.start()
        for copy in copies:
            copy.wait()

    for k in range(members):
        cols = slice(k * size, (k + 1) * size)
        wanted = place[core * members + k, tile] >= 0

        def store(values):
            for j, out in enumerate(outs):

                @pl.when(step == j)
                def _():
                    out[:, cols] = values

        @pl.when(wanted)
        def _():
            first = panel[k, pl.ds(core * half, half)].reshape(half * size, size)
            second = panel[k, pl.ds((1 - core) * half, half)].reshape(half * size, size)
            values = jnp.dot(own_ref[...], first, preferred_element_type=F32)
            values += jnp.dot(other_ref[...], second, preferred_element_type=F32)
            level = level_of(jnp.max(jnp.abs(values), axis=0, keepdims=True))
            tail = jnp.broadcast_to(level, (16, size)).astype(jnp.int32).astype(I16)
            store(jnp.concatenate([code(values, level), tail], axis=0))

        @pl.when(jnp.logical_not(wanted))
        def _():
            store(jnp.zeros((size + 16, size), I16))


def diagonal_kernel(place, where, *refs):
    count = NH * NY
    coded, parts, (d_ref, block) = refs[:count], refs[count : 2 * count], refs[2 * count :]
    _, members, _, size = parts[0].shape
    core, group, h, y = where[1], where[2], where[5], where[6]
    block[...] = jnp.zeros_like(block)
    for side in range(NH):
        for hop, shift in enumerate(RING):
            tile = lax.rem(h + side, NH) * NY + lax.rem(y + shift, NY)
            q_ref, ref = coded[side * NY + shift], parts[side * NY + hop]
            for k in range(members):
                cols = slice(k * size, (k + 1) * size)

                @pl.when(place[core * members + k, group * count + tile] >= 0)
                def _():
                    own = ref[:, k].reshape(size, size)
                    rest = plain(q_ref[:size, cols])
                    high = rest.astype(BF16)
                    low = (rest - high.astype(F32)).astype(BF16)
                    total = sum(
                        lax.dot_general(
                            own, term, (((0,), (0,)), ((), ())), preferred_element_type=F32
                        )
                        for term in (high, low)
                    )
                    block[:, cols] -= total * scale_of(plain(q_ref[size : size + 16, cols])[:1])

    values = block[...]
    level = level_of(jnp.max(jnp.abs(values), keepdims=True))
    width = values.shape[1] // 2
    for i in range(2):
        d_ref[i, :, :width] = code(values[:, i * width : (i + 1) * width], level)
        d_ref[i, :, width:] = jnp.broadcast_to(level, (size, LANES)).astype(jnp.int32).astype(I16)


def finish_kernel(place, where, *refs):
    parts, (u_ref, swap_ref) = refs[:-2], refs[-2:]
    sources = len(parts)
    slab, width = u_ref.shape
    size = 2 * slab
    members = width // size
    chip, core, group = where[0], where[1], where[2]
    mine = group * sources + chip
    for k in range(members):
        cols = slice(k * size, (k + 1) * size)
        total = jnp.zeros((size, size), F32)
        for ref in parts:
            scale = scale_of(plain(ref[size : size + 16, cols])[:1])
            total += plain(ref[:size, cols]) * scale
        keep = place[core * members + k, mine] >= 0
        rounded = jnp.where(keep, -total, jnp.zeros_like(total)).astype(BF16)
        first = core == 0
        u_ref[:, cols] = jnp.where(first, rounded[:slab], rounded[slab:])
        swap_ref[:, cols] = jnp.where(first, rounded[slab:], rounded[:slab])


def piece_kernel(q_ref, o_ref):
    width = q_ref.shape[2] - LANES
    scale = scale_of(plain(q_ref[:, :, width:]))
    sums = [
        jnp.sum(plain(q_ref[:, :, i : i + LANES]) * scale, axis=0) for i in range(0, width, LANES)
    ]
    values = jnp.concatenate(sums, axis=1)
    level = level_of(jnp.max(jnp.abs(values), keepdims=True))
    coded = jnp.concatenate(
        [
            code(values, level),
            jnp.broadcast_to(level, (values.shape[0], LANES)).astype(jnp.int32).astype(I16),
        ],
        axis=1,
    )
    for j in range(o_ref.shape[0]):
        o_ref[j] = coded


def total_kernel(q_ref, inverse_ref, o_ref):
    pieces, cores, depth, _ = q_ref.shape
    supers, size, _ = inverse_ref.shape
    width = q_ref.shape[3] - LANES
    count = pieces // 2
    for c in range(cores):
        for i in range(2):
            rows = slice(i * count, (i + 1) * count)
            scale = scale_of(plain(q_ref[rows, c, :, width:]))
            for t in range(width // LANES):
                lane = (i * width + t * LANES) % size
                k = c * (supers // cores) + (i * width + t * LANES) // size
                values = plain(q_ref[rows, c, :, t * LANES : (t + 1) * LANES]) * scale
                values = values.reshape(count * depth, LANES)
                o_ref[k, :, lane : lane + LANES] = (
                    inverse_ref[k, :, lane : lane + LANES] - values
                )


def spread(own, axis, up):
    below = lax.ppermute(own, axis, UP)
    above = lax.ppermute(own, axis, DOWN)
    far = lax.ppermute(below, axis, UP) if up else lax.ppermute(above, axis, DOWN)
    return [own, below, above, far]


RING = (0, 3, 1, 2)


def update(ancestor_inv, lfactor, struct, validity, diag_inverse):
    rows, cols = ancestor_inv.shape
    entries, size, supers, _ = lfactor.shape
    groups = NX * NL
    chips = NH * NY
    part = size // groups
    members = supers // NC
    width = members * size
    group = lax.axis_index(XL)
    chip = lax.axis_index(HY)
    core = lax.axis_index("c")
    listed = struct.shape[1]
    tiles = rows * groups // size
    window = tiles // chips
    smem = pl.BlockSpec(memory_space=pltpu.SMEM)
    vmem = pl.BlockSpec(memory_space=pltpu.VMEM)

    other = lax.ppermute(ancestor_inv, "c", CORE_SWAP)

    hits = (struct[:, :, None] == jnp.arange(tiles, dtype=jnp.int32)) & (validity[:, :, None] > 0)
    position = jnp.arange(listed, dtype=jnp.int32)[None, :, None]
    place = jnp.max(jnp.where(hits, position, -1), axis=1)
    where = jnp.stack([chip, core, group] + [lax.axis_index(a) for a in ("x", "l", "h", "y")])

    share = jnp.transpose(lfactor, (0, 2, 1, 3))
    share = lax.dynamic_slice_in_dim(share, group * part, part, 2)
    share = share.reshape(entries, NC, members, part, size)
    share = jnp.transpose(share, (1, 0, 2, 3, 4))
    share = jnp.broadcast_to(share[None], (chips,) + share.shape)
    share = share.reshape((chips * NC,) + share.shape[2:])
    share = lax.all_to_all(share, ("h", "y", "c"), split_axis=0, concat_axis=0, tiled=True)
    share = share.reshape(listed, members, part, size)

    block = jax.ShapeDtypeStruct((members, window, part, size), BF16)
    near, own = pl.pallas_call(
        pick_kernel,
        out_shape=[block, jax.ShapeDtypeStruct((groups, members, part, size), BF16)],
        in_specs=[smem, smem, vmem],
        out_specs=[vmem] * 2,
        name="pick",
    )(place, where, share)
    across = lax.ppermute(near, "l", CORE_SWAP)
    window_parts = spread(near, "x", True)
    window_parts += spread(across, "x", False)
    own = lax.all_to_all(own, XL, split_axis=0, concat_axis=0, tiled=True)
    across = lax.ppermute(own, "h", CORE_SWAP)
    row_parts = spread(own, "y", True)
    row_parts += spread(across, "y", False)

    def row_tile(j, _, where):
        return lax.rem(where[5] + j // NY, NH) * NY + lax.rem(where[6] + j, NY), 0

    coded = pl.pallas_call(
        product_kernel,
        out_shape=[jax.ShapeDtypeStruct((size + 16, width), I16)] * chips,
        grid_spec=pltpu.PrefetchScalarGridSpec(
            num_scalar_prefetch=2,
            grid=(chips,),
            in_specs=[pl.BlockSpec((size, cols), row_tile)] * 2
            + [pl.BlockSpec(memory_space=pl.ANY)] * len(window_parts),
            out_specs=[vmem] * chips,
            scratch_shapes=[
                pltpu.VMEM((members, window, groups, part, size), BF16),
                pltpu.SemaphoreType.DMA((len(window_parts),)),
            ],
        ),
        name="product",
    )(place, where, ancestor_inv, other, *window_parts)
    pieces = groups * chips
    depth = 2 * size // pieces
    reach = width // 2 + LANES
    diag = pl.pallas_call(
        diagonal_kernel,
        out_shape=jax.ShapeDtypeStruct((2, size, reach), I16),
        in_specs=[smem, smem] + [vmem] * (chips + len(row_parts)),
        out_specs=vmem,
        scratch_shapes=[pltpu.VMEM((size, width), F32)],
        name="diagonal",
    )(place, where, *coded, *row_parts)

    sums = [coded[0]]
    for shifts in ((6, 5, 7), (2, 4, 1, 3)):
        for j in shifts:
            to = [
                (h * NY + y, (h + j // NY) % NH * NY + (y + j) % NY)
                for h in range(NH)
                for y in range(NY)
            ]
            sums.append(lax.ppermute(coded[j], HY, to))
    slab = jax.ShapeDtypeStruct((size // NC, width), BF16)
    mine, theirs = pl.pallas_call(
        finish_kernel,
        out_shape=[slab, slab],
        in_specs=[smem, smem] + [vmem] * len(sums),
        out_specs=[vmem] * 2,
        name="finish",
    )(place, where, *sums)

    theirs = lax.ppermute(theirs, "c", CORE_SWAP)
    column_block = jnp.where(
        core == 0,
        jnp.concatenate([mine, theirs], axis=1),
        jnp.concatenate([theirs, mine], axis=1),
    )

    diag = diag.reshape(pieces, depth, reach)
    diag = lax.all_to_all(diag, CHIPS, split_axis=0, concat_axis=0, tiled=True)
    piece = pl.pallas_call(
        piece_kernel,
        out_shape=jax.ShapeDtypeStruct((pieces * NC, depth, reach), I16),
        in_specs=[vmem],
        out_specs=vmem,
        name="piece",
    )(diag)
    whole = lax.all_to_all(piece, CHIPS + ("c",), split_axis=0, concat_axis=0, tiled=True)
    diagonal = pl.pallas_call(
        total_kernel,
        out_shape=jax.ShapeDtypeStruct(diag_inverse.shape, F32),
        in_specs=[vmem, vmem],
        out_specs=vmem,
        name="total",
    )(whole.reshape(pieces, NC, depth, reach), diag_inverse)
    return column_block, diagonal


def solution(mesh):
    fine = Mesh(mesh.devices.reshape(NX, NL, NH, NY, NC), ("x", "l", "h", "y", "c"))
    return jax.shard_map(
        update,
        mesh=fine,
        in_specs=(P(XL, ("h", "y", "c")), P(("h", "y", "c")), P(), P(), P()),
        out_specs=(P(("x", "l", "h", "y", "c")), P()),
        check_vma=False,
    )
```

profile of v0, /device:TPU:1, one launch (start us, length us, event | category | flops | bytes accessed | tf_op | source)
XLA Modules:
  0.0 195.0 jit_solution(13286477903472809990)
XLA Ops:
  0.6 1.5 collective-permute-start
  2.1 1.3 broadcast_in_dim.24
  3.5 9.4 %all-to-all-start = ((bf16[16,2,3,32,256]{4,3,2,1,0:T(8,128)(2,1)}), bf16[16,2,3,32,256]{4,3,2,1,0:T(8,128)(2,1)S(1)}, u32[]{:S(2)}, u32[]{:S(2)}) async-start(bf16[16,2,3,32,256]{4,3,2,1,0:T(8,128)(2,1)} %bitcast.17), calls=%async_computation | async-start | bytes 3145728 | tf_op jit(solution)/shard_map/all_to_all | solution.py:240
  12.8 0.6 stack.31.where
  13.4 0.7 select_reduce_fusion.place
  14.2 21.6 %all-to-all-done = bf16[16,2,3,32,256]{4,3,2,1,0:T(8,128)(2,1)S(1)} async-done(((bf16[16,2,3,32,256]{4,3,2,1,0:T(8,128)(2,1)}), bf16[16,2,3,32,256]{4,3,2,1,0:T(8,128)(2,1)S(1)}, u32[]{:S(2)}, u32[]{:S(2)}) %all-to-all-start) | async-done | bytes 1572896 | tf_op jit(solution)/shard_map/all_to_all | solution.py:240
  35.7 1.1 copy-done.1
  36.9 2.5 %pick.1 = (bf16[3,8,32,256]{3,2,1,0:T(8,128)(2,1)}, bf16[8,3,32,256]{3,2,1,0:T(8,128)(2,1)}) custom-call(s32[6,64]{1,0:T(8,128)} %select_reduce_fusion.place, s32[7]{0:T(128)} %stack.31.where, bf16[32,3,32,256]{3,2,1,0:T(8,128)(2,1)} %bitcast.16), custom_call_target="tpu_custom_call" | custom-call | tf_op jit(solution)/shard_map/pick/pallas_call | solution.py:244
  39.3 0.7 collective-permute-start.4
  40.1 1.2 collective-permute-start.1
  41.3 4.2 %all-to-all-start.1 = ((bf16[8,3,32,256]{3,2,1,0:T(8,128)(2,1)}), bf16[8,3,32,256]{3,2,1,0:T(8,128)(2,1)S(1)}, u32[]{:S(2)}, u32[]{:S(2)}) async-start(bf16[8,3,32,256]{3,2,1,0:T(8,128)(2,1)} %get-tuple-element.25), calls=%async_computation.1 | async-start | bytes 786432 | tf_op jit(solution)/shard_map/all_to_all | solution.py:254
  45.5 2.7 %collective-permute-start.2 = (bf16[3,8,32,256]{3,2,1,0:T(8,128)(2,1)}, bf16[3,8,32,256]{3,2,1,0:T(8,128)(2,1)S(1)}, u32[]{:S(2)}, u32[]{:S(2)}) collective-permute-start(bf16[3,8,32,256]{3,2,1,0:T(8,128)(2,1)} %get-tuple-element.14.refs_0_), channel_id=1, source_target_pairs={{0,96},{32,0},{64,32},{96,64},{1,97},{33,1},{65,33},{97,65},{2,98}... | collective-permute-start | bytes 1179656 | tf_op jit(solution)/shard_map/ppermute | solution.py:202
  48.1 8.2 %all-to-all-done.1.refs_8_ = bf16[8,3,32,256]{3,2,1,0:T(8,128)(2,1)S(1)} async-done(((bf16[8,3,32,256]{3,2,1,0:T(8,128)(2,1)}), bf16[8,3,32,256]{3,2,1,0:T(8,128)(2,1)S(1)}, u32[]{:S(2)}, u32[]{:S(2)}) %all-to-all-start.1) | async-done | bytes 393248 | tf_op jit(solution)/shard_map/all_to_all | solution.py:254
  56.3 1.2 collective-permute-start.19
  57.9 1.1 collective-permute-done.2.refs_2_
  59.0 1.4 collective-permute-start.5
  60.4 6.2 %collective-permute-done.19.refs_12_ = bf16[8,3,32,256]{3,2,1,0:T(8,128)(2,1)} collective-permute-done((bf16[8,3,32,256]{3,2,1,0:T(8,128)(2,1)S(1)}, bf16[8,3,32,256]{3,2,1,0:T(8,128)(2,1)}, u32[]{:S(2)}, u32[]{:S(2)}) %collective-permute-start.19) | collective-permute-done | bytes 393248 | tf_op jit(solution)/shard_map/ppermute | solution.py:255
  66.7 0.6 collective-permute-done.16.refs_9_
  67.2 2.6 %collective-permute-start.21 = (bf16[8,3,32,256]{3,2,1,0:T(8,128)(2,1)}, bf16[8,3,32,256]{3,2,1,0:T(8,128)(2,1)}, u32[]{:S(2)}, u32[]{:S(2)}) collective-permute-start(bf16[8,3,32,256]{3,2,1,0:T(8,128)(2,1)} %collective-permute-done.19.refs_12_), channel_id=1, source_target_pairs={{0,6},{2,0},{4,2},{6,4},{1,7},{3,1},{5,3},{7,5},{8,14},{10,8},{12,... | collective-permute-start | bytes 1179656 | tf_op jit(solution)/shard_map/ppermute | solution.py:202
  69.8 2.7 %collective-permute-start.7 = (bf16[3,8,32,256]{3,2,1,0:T(8,128)(2,1)S(1)}, bf16[3,8,32,256]{3,2,1,0:T(8,128)(2,1)S(1)}, u32[]{:S(2)}, u32[]{:S(2)}) collective-permute-start(bf16[3,8,32,256]{3,2,1,0:T(8,128)(2,1)S(1)} %collective-permute-done.6.refs_6_), channel_id=1, source_target_pairs={{0,96},{32,0},{64,32},{96,64},{1,97},{33,1},{65,33},{97,65},{2,98}... | collective-permute-start | bytes 1179656 | tf_op jit(solution)/shard_map/ppermute | solution.py:203
  72.6 5.1 %collective-permute-done.3.refs_3_ = bf16[3,8,32,256]{3,2,1,0:T(8,128)(2,1)S(1)} collective-permute-done((bf16[3,8,32,256]{3,2,1,0:T(8,128)(2,1)S(1)}, bf16[3,8,32,256]{3,2,1,0:T(8,128)(2,1)S(1)}, u32[]{:S(2)}, u32[]{:S(2)}) %collective-permute-start.3) | collective-permute-done | bytes 393248 | tf_op jit(solution)/shard_map/ppermute | solution.py:203
  77.6 0.6 collective-permute-start.20
  78.8 2.2 %collective-permute-start.22 = (bf16[8,3,32,256]{3,2,1,0:T(8,128)(2,1)}, bf16[8,3,32,256]{3,2,1,0:T(8,128)(2,1)}, u32[]{:S(2)}, u32[]{:S(2)}) collective-permute-start(bf16[8,3,32,256]{3,2,1,0:T(8,128)(2,1)} %collective-permute-done.21.refs_14_), channel_id=1, source_target_pairs={{0,6},{2,0},{4,2},{6,4},{1,7},{3,1},{5,3},{7,5},{8,14},{10,8},{12,... | collective-permute-start | bytes 1179656 | tf_op jit(solution)/shard_map/ppermute | solution.py:203
  81.0 12.9 %product.1 = (s16[272,768]{1,0:T(8,128)(2,1)}, s16[272,768]{1,0:T(8,128)(2,1)}, s16[272,768]{1,0:T(8,128)(2,1)}, s16[272,768]{1,0:T(8,128)(2,1)}, s16[272,768]{1...) custom-call(s32[6,64]{1,0:T(8,128)} %select_reduce_fusion.place, ...), custom_call_target="tpu_custom_call" | custom-call | tf_op jit(solution)/shard_map/product/pallas_call | solution.py:262
  94.0 1.6 collective-permute-done.18.refs_11_
  95.6 5.9 %diagonal.1 = s16[2,256,512]{2,1,0:T(8,128)(2,1)} custom-call(s32[6,64]{1,0:T(8,128)} %select_reduce_fusion.place, s32[7]{0:T(128)} %stack.31.where, s16[272,768]{1,0:T(8,128)(2,1)} %get-tuple-element.15.refs_0_, s16[272,768]{1,0:T(8,128)(2,1)} %get-tuple-element.21.refs_1_, s16[272,768]{1,0:T(8,128)(2,1)} %get-tuple-element.19.refs_2_, ...), custom_call_target="tpu_custom_call" | custom-call | tf_op jit(solution)/shard_map/diagonal/pallas_call | solution.py:281
  101.4 8.6 %all-to-all-start.2 = ((s16[64,8,512]{2,1,0:T(8,128)(2,1)}), s16[64,8,512]{2,1,0:T(8,128)(2,1)S(1)}, u32[]{:S(2)}, u32[]{:S(2)}) async-start(s16[64,8,512]{2,1,0:T(8,128)(2,1)} %bitcast.19), calls=%async_computation.2 | async-start | bytes 1048576 | tf_op jit(solution)/shard_map/all_to_all | solution.py:316
  110.0 4.7 %collective-permute-start.10 = (s16[272,768]{1,0:T(8,128)(2,1)}, s16[272,768]{1,0:T(8,128)(2,1)}, u32[]{:S(2)}, u32[]{:S(2)}) collective-permute-start(s16[272,768]{1,0:T(8,128)(2,1)} %get-tuple-element.18.refs_7_), channel_id=1, source_target_pairs={{0,14},{2,8},{4,10},{6,12},{8,6},{10,0},{12,2},{14,4},{1,15},{3,9}... | collective-permute-start | bytes 1253384 | tf_op jit(solution)/shard_map/ppermute | solution.py:298
  114.7 0.6 collective-permute-start.11
  115.3 5.7 %all-to-all-done.2.q_ref = s16[64,8,512]{2,1,0:T(8,128)(2,1)S(1)} async-done(((s16[64,8,512]{2,1,0:T(8,128)(2,1)}), s16[64,8,512]{2,1,0:T(8,128)(2,1)S(1)}, u32[]{:S(2)}, u32[]{:S(2)}) %all-to-all-start.2) | async-done | bytes 524320 | tf_op jit(solution)/shard_map/all_to_all | solution.py:316
  121.0 0.8 copy-done.3
  121.8 2.4 %piece.1 = s16[128,8,512]{2,1,0:T(8,128)(2,1)} custom-call(s16[64,8,512]{2,1,0:T(8,128)(2,1)} %copy-done.3), custom_call_target="tpu_custom_call" | custom-call | tf_op jit(solution)/shard_map/piece/pallas_call | solution.py:317
  124.2 15.1 %all-to-all-start.3 = ((s16[128,8,512]{2,1,0:T(8,128)(2,1)}), s16[128,8,512]{2,1,0:T(8,128)(2,1)S(1)}, u32[]{:S(2)}, u32[]{:S(2)}) async-start(s16[128,8,512]{2,1,0:T(8,128)(2,1)} %piece.1), calls=%async_computation.3 | async-start | bytes 2097152 | tf_op jit(solution)/shard_map/all_to_all | solution.py:324
  139.3 3.3 %collective-permute-start.12 = (s16[272,768]{1,0:T(8,128)(2,1)}, s16[272,768]{1,0:T(8,128)(2,1)S(1)}, u32[]{:S(2)}, u32[]{:S(2)}) collective-permute-start(s16[272,768]{1,0:T(8,128)(2,1)} %get-tuple-element.20.refs_4_), channel_id=1, source_target_pairs={{0,8},{2,10},{4,12},{6,14},{8,0},{10,2},{12,4},{14,6},{1,9},{3,11}... | collective-permute-start | bytes 1253384 | tf_op jit(solution)/shard_map/ppermute | solution.py:298
  142.6 1.2 collective-permute-start.13
  143.9 1.4 collective-permute-start.14
  145.3 1.4 collective-permute-start.8
  146.7 3.0 %collective-permute-start.9 = (s16[272,768]{1,0:T(8,128)(2,1)S(1)}, s16[272,768]{1,0:T(8,128)(2,1)}, u32[]{:S(2)}, u32[]{:S(2)}) collective-permute-start(s16[272,768]{1,0:T(8,128)(2,1)S(1)} %copy-done.5), channel_id=1, source_target_pairs={{0,10},{2,12},{4,14},{6,8},{8,2},{10,4},{12,6},{14,0},{1,11},{3,13... | collective-permute-start | bytes 1253384 | tf_op jit(solution)/shard_map/ppermute | solution.py:298
  149.7 13.4 %collective-permute-done.12.refs_5_ = s16[272,768]{1,0:T(8,128)(2,1)S(1)} collective-permute-done((s16[272,768]{1,0:T(8,128)(2,1)}, s16[272,768]{1,0:T(8,128)(2,1)S(1)}, u32[]{:S(2)}, u32[]{:S(2)}) %collective-permute-start.12) | collective-permute-done | bytes 417824 | tf_op jit(solution)/shard_map/ppermute | solution.py:298
  163.1 11.2 %collective-permute-done.8.refs_1_ = s16[272,768]{1,0:T(8,128)(2,1)S(1)} collective-permute-done((s16[272,768]{1,0:T(8,128)(2,1)S(1)}, s16[272,768]{1,0:T(8,128)(2,1)S(1)}, u32[]{:S(2)}, u32[]{:S(2)}) %collective-permute-start.8) | collective-permute-done | bytes 417824 | tf_op jit(solution)/shard_map/ppermute | solution.py:298
  174.3 0.7 copy-done.10
  175.1 8.1 %collective-permute-done.9.refs_2_ = s16[272,768]{1,0:T(8,128)(2,1)} collective-permute-done((s16[272,768]{1,0:T(8,128)(2,1)S(1)}, s16[272,768]{1,0:T(8,128)(2,1)}, u32[]{:S(2)}, u32[]{:S(2)}) %collective-permute-start.9) | collective-permute-done | bytes 417824 | tf_op jit(solution)/shard_map/ppermute | solution.py:298
  183.2 3.5 %finish.1 = (bf16[128,768]{1,0:T(8,128)(2,1)}, bf16[128,768]{1,0:T(8,128)(2,1)}) custom-call(s32[6,64]{1,0:T(8,128)} %select_reduce_fusion.place, s32[7]{0:T(128)} %stack.31.where, s16[272,768]{1,0:T(8,128)(2,1)} %get-tuple-element.15.refs_0_, s16[272,768]{1,0:T(8,128)(2,1)} %copy-done.10, s16[272,768]{1,0:T(8,128)(2,1)} %collective-permute-done.9.refs_2_, ...), custom_call_target="tpu_custom_call" | custom-call | tf_op jit(solution)/shard_map/finish/pallas_call | solution.py:300
  186.7 1.0 collective-permute-start.15
  187.7 1.3 collective-permute-done.15
  189.0 1.9 maximum_select_fusion
  190.8 1.0 copy-done.2
  191.8 3.2 %total.1 = f32[6,256,256]{2,1,0:T(8,128)} custom-call(s16[64,2,8,512]{3,2,1,0:T(8,128)(2,1)} %bitcast.18, f32[6,256,256]{2,1,0:T(8,128)} %inverse_ref.1), custom_call_target="tpu_custom_call" | custom-call | tf_op jit(solution)/shard_map/total/pallas_call | solution.py:325
  (59 shorter events, 1.2 us)
Async XLA Ops:
  0.6 1.5 copy-start
  0.6 80.3 %collective-permute-start = (bf16[2048,1024]{1,0:T(8,128)(2,1)}, bf16[2048,1024]{1,0:T(8,128)(2,1)}, u32[]{:S(2)}, u32[]{:S(2)}) collective-permute-start(bf16[2048,1024]{1,0:T(8,128)(2,1)} %own_ref.1), channel_id=1, source_target_pairs={{0,1},{1,0},{2,3},{3,2},{4,5},{5,4},{6,7},{7,6},{8,9},{9,8},{10,11... | collective-permute-start | bytes 12582920 | tf_op jit(solution)/shard_map/ppermute | solution.py:227
  3.5 9.9 %copy-start.18 = (s32[6,32]{1,0:T(8,128)S(1)}, s32[6,32]{1,0:T(8,128)}, u32[]{:S(2)}) copy-start(s32[6,32]{1,0:T(8,128)} %param.8) | copy-start | bytes 2308
  3.5 9.9 %copy-start.19 = (s32[6,32]{1,0:T(8,128)S(1)}, s32[6,32]{1,0:T(8,128)}, u32[]{:S(2)}) copy-start(s32[6,32]{1,0:T(8,128)} %param.7) | copy-start | bytes 2308
  3.5 32.2 %all-to-all-start = ((bf16[16,2,3,32,256]{4,3,2,1,0:T(8,128)(2,1)}), bf16[16,2,3,32,256]{4,3,2,1,0:T(8,128)(2,1)S(1)}, u32[]{:S(2)}, u32[]{:S(2)}) async-start(bf16[16,2,3,32,256]{4,3,2,1,0:T(8,128)(2,1)} %bitcast.17), calls=%async_computation | async-start | bytes 3145728 | tf_op jit(solution)/shard_map/all_to_all | solution.py:240
  35.7 1.1 copy-start.1
  39.3 18.1 %collective-permute-start.4 = (bf16[3,8,32,256]{3,2,1,0:T(8,128)(2,1)}, bf16[3,8,32,256]{3,2,1,0:T(8,128)(2,1)S(1)}, u32[]{:S(2)}, u32[]{:S(2)}) collective-permute-start(bf16[3,8,32,256]{3,2,1,0:T(8,128)(2,1)} %get-tuple-element.14.refs_0_), channel_id=1, source_target_pairs={{0,16},{16,0},{1,17},{17,1},{2,18},{18,2},{3,19},{19,3},{4,20},{20... | collective-permute-start | bytes 1179656 | tf_op jit(solution)/shard_map/ppermute | solution.py:251
  40.1 17.8 %collective-permute-start.1 = (bf16[3,8,32,256]{3,2,1,0:T(8,128)(2,1)}, bf16[3,8,32,256]{3,2,1,0:T(8,128)(2,1)S(1)}, u32[]{:S(2)}, u32[]{:S(2)}) collective-permute-start(bf16[3,8,32,256]{3,2,1,0:T(8,128)(2,1)} %get-tuple-element.14.refs_0_), channel_id=1, source_target_pairs={{0,32},{32,64},{64,96},{96,0},{1,33},{33,65},{65,97},{97,1},{2,34}... | collective-permute-start | bytes 1179656 | tf_op jit(solution)/shard_map/ppermute | solution.py:201
  41.3 15.0 %all-to-all-start.1 = ((bf16[8,3,32,256]{3,2,1,0:T(8,128)(2,1)}), bf16[8,3,32,256]{3,2,1,0:T(8,128)(2,1)S(1)}, u32[]{:S(2)}, u32[]{:S(2)}) async-start(bf16[8,3,32,256]{3,2,1,0:T(8,128)(2,1)} %get-tuple-element.25), calls=%async_computation.1 | async-start | bytes 786432 | tf_op jit(solution)/shard_map/all_to_all | solution.py:254
  45.5 13.5 %collective-permute-start.2 = (bf16[3,8,32,256]{3,2,1,0:T(8,128)(2,1)}, bf16[3,8,32,256]{3,2,1,0:T(8,128)(2,1)S(1)}, u32[]{:S(2)}, u32[]{:S(2)}) collective-permute-start(bf16[3,8,32,256]{3,2,1,0:T(8,128)(2,1)} %get-tuple-element.14.refs_0_), channel_id=1, source_target_pairs={{0,96},{32,0},{64,32},{96,64},{1,97},{33,1},{65,33},{97,65},{2,98}... | collective-permute-start | bytes 1179656 | tf_op jit(solution)/shard_map/ppermute | solution.py:202
  56.3 37.6 %copy-start.4 = (bf16[8,3,32,256]{3,2,1,0:T(8,128)(2,1)}, bf16[8,3,32,256]{3,2,1,0:T(8,128)(2,1)S(1)}, u32[]{:S(2)}) copy-start(bf16[8,3,32,256]{3,2,1,0:T(8,128)(2,1)S(1)} %all-to-all-done.1.refs_8_) | copy-start | bytes 1179652
  56.3 10.4 %collective-permute-start.19 = (bf16[8,3,32,256]{3,2,1,0:T(8,128)(2,1)S(1)}, bf16[8,3,32,256]{3,2,1,0:T(8,128)(2,1)}, u32[]{:S(2)}, u32[]{:S(2)}) collective-permute-start(bf16[8,3,32,256]{3,2,1,0:T(8,128)(2,1)S(1)} %all-to-all-done.1.refs_8_), channel_id=1, source_target_pairs={{0,8},{8,0},{1,9},{9,1},{2,10},{10,2},{3,11},{11,3},{4,12},{12,4},... | collective-permute-start | bytes 1179656 | tf_op jit(solution)/shard_map/ppermute | solution.py:255
  57.5 23.5 %copy-start.11 = (bf16[3,8,32,256]{3,2,1,0:T(8,128)(2,1)}, bf16[3,8,32,256]{3,2,1,0:T(8,128)(2,1)S(1)}, u32[]{:S(2)}) copy-start(bf16[3,8,32,256]{3,2,1,0:T(8,128)(2,1)S(1)} %collective-permute-done.4.refs_4_) | copy-start | bytes 1179652
  57.5 9.8 %collective-permute-start.16 = (bf16[8,3,32,256]{3,2,1,0:T(8,128)(2,1)S(1)}, bf16[8,3,32,256]{3,2,1,0:T(8,128)(2,1)}, u32[]{:S(2)}, u32[]{:S(2)}) collective-permute-start(bf16[8,3,32,256]{3,2,1,0:T(8,128)(2,1)S(1)} %all-to-all-done.1.refs_8_), channel_id=1, source_target_pairs={{0,2},{2,4},{4,6},{6,0},{1,3},{3,5},{5,7},{7,1},{8,10},{10,12},{12... | collective-permute-start | bytes 1179656 | tf_op jit(solution)/shard_map/ppermute | solution.py:201
  57.9 23.2 %copy-start.12 = (bf16[3,8,32,256]{3,2,1,0:T(8,128)(2,1)}, bf16[3,8,32,256]{3,2,1,0:T(8,128)(2,1)S(1)}, u32[]{:S(2)}) copy-start(bf16[3,8,32,256]{3,2,1,0:T(8,128)(2,1)S(1)} %collective-permute-done.1.refs_1_) | copy-start | bytes 1179652
  57.9 12.0 %collective-permute-start.6 = (bf16[3,8,32,256]{3,2,1,0:T(8,128)(2,1)S(1)}, bf16[3,8,32,256]{3,2,1,0:T(8,128)(2,1)S(1)}, u32[]{:S(2)}, u32[]{:S(2)}) collective-permute-start(bf16[3,8,32,256]{3,2,1,0:T(8,128)(2,1)S(1)} %collective-permute-done.4.refs_4_), channel_id=1, source_target_pairs={{0,96},{32,0},{64,32},{96,64},{1,97},{33,1},{65,33},{97,65},{2,98}... | collective-permute-start | bytes 1179656 | tf_op jit(solution)/shard_map/ppermute | solution.py:202
  59.0 22.0 %copy-start.13 = (bf16[3,8,32,256]{3,2,1,0:T(8,128)(2,1)}, bf16[3,8,32,256]{3,2,1,0:T(8,128)(2,1)S(1)}, u32[]{:S(2)}) copy-start(bf16[3,8,32,256]{3,2,1,0:T(8,128)(2,1)S(1)} %collective-permute-done.2.refs_2_) | copy-start | bytes 1179652
  59.0 13.5 %collective-permute-start.5 = (bf16[3,8,32,256]{3,2,1,0:T(8,128)(2,1)S(1)}, bf16[3,8,32,256]{3,2,1,0:T(8,128)(2,1)S(1)}, u32[]{:S(2)}, u32[]{:S(2)}) collective-permute-start(bf16[3,8,32,256]{3,2,1,0:T(8,128)(2,1)S(1)} %collective-permute-done.4.refs_4_), channel_id=1, source_target_pairs={{0,32},{32,64},{64,96},{96,0},{1,33},{33,65},{65,97},{97,1},{2,34}... | collective-permute-start | bytes 1179656 | tf_op jit(solution)/shard_map/ppermute | solution.py:201
  66.7 11.0 %collective-permute-start.3 = (bf16[3,8,32,256]{3,2,1,0:T(8,128)(2,1)S(1)}, bf16[3,8,32,256]{3,2,1,0:T(8,128)(2,1)S(1)}, u32[]{:S(2)}, u32[]{:S(2)}) collective-permute-start(bf16[3,8,32,256]{3,2,1,0:T(8,128)(2,1)S(1)} %collective-permute-done.1.refs_1_), channel_id=1, source_target_pairs={{0,32},{32,64},{64,96},{96,0},{1,33},{33,65},{65,97},{97,1},{2,34}... | collective-permute-start | bytes 1179656 | tf_op jit(solution)/shard_map/ppermute | solution.py:203
  67.2 11.0 %collective-permute-start.21 = (bf16[8,3,32,256]{3,2,1,0:T(8,128)(2,1)}, bf16[8,3,32,256]{3,2,1,0:T(8,128)(2,1)}, u32[]{:S(2)}, u32[]{:S(2)}) collective-permute-start(bf16[8,3,32,256]{3,2,1,0:T(8,128)(2,1)} %collective-permute-done.19.refs_12_), channel_id=1, source_target_pairs={{0,6},{2,0},{4,2},{6,4},{1,7},{3,1},{5,3},{7,5},{8,14},{10,8},{12,... | collective-permute-start | bytes 1179656 | tf_op jit(solution)/shard_map/ppermute | solution.py:202
  69.8 11.2 %copy-start.14 = (bf16[3,8,32,256]{3,2,1,0:T(8,128)(2,1)}, bf16[3,8,32,256]{3,2,1,0:T(8,128)(2,1)S(1)}, u32[]{:S(2)}) copy-start(bf16[3,8,32,256]{3,2,1,0:T(8,128)(2,1)S(1)} %collective-permute-done.6.refs_6_) | copy-start | bytes 1179652
  69.8 9.0 %collective-permute-start.7 = (bf16[3,8,32,256]{3,2,1,0:T(8,128)(2,1)S(1)}, bf16[3,8,32,256]{3,2,1,0:T(8,128)(2,1)S(1)}, u32[]{:S(2)}, u32[]{:S(2)}) collective-permute-start(bf16[3,8,32,256]{3,2,1,0:T(8,128)(2,1)S(1)} %collective-permute-done.6.refs_6_), channel_id=1, source_target_pairs={{0,96},{32,0},{64,32},{96,64},{1,97},{33,1},{65,33},{97,65},{2,98}... | collective-permute-start | bytes 1179656 | tf_op jit(solution)/shard_map/ppermute | solution.py:203
  72.5 6.3 %copy-start.15 = (bf16[3,8,32,256]{3,2,1,0:T(8,128)(2,1)}, bf16[3,8,32,256]{3,2,1,0:T(8,128)(2,1)S(1)}, u32[]{:S(2)}) copy-start(bf16[3,8,32,256]{3,2,1,0:T(8,128)(2,1)S(1)} %collective-permute-done.5.refs_5_) | copy-start | bytes 1179652
  72.5 21.4 %collective-permute-start.17 = (bf16[8,3,32,256]{3,2,1,0:T(8,128)(2,1)S(1)}, bf16[8,3,32,256]{3,2,1,0:T(8,128)(2,1)}, u32[]{:S(2)}, u32[]{:S(2)}) collective-permute-start(bf16[8,3,32,256]{3,2,1,0:T(8,128)(2,1)S(1)} %all-to-all-done.1.refs_8_), channel_id=1, source_target_pairs={{0,6},{2,0},{4,2},{6,4},{1,7},{3,1},{5,3},{7,5},{8,14},{10,8},{12,... | collective-permute-start | bytes 1179656 | tf_op jit(solution)/shard_map/ppermute | solution.py:202
  77.6 3.3 %copy-start.16 = (bf16[3,8,32,256]{3,2,1,0:T(8,128)(2,1)}, bf16[3,8,32,256]{3,2,1,0:T(8,128)(2,1)S(1)}, u32[]{:S(2)}) copy-start(bf16[3,8,32,256]{3,2,1,0:T(8,128)(2,1)S(1)} %collective-permute-done.3.refs_3_) | copy-start | bytes 1179652
  77.6 16.3 %collective-permute-start.20 = (bf16[8,3,32,256]{3,2,1,0:T(8,128)(2,1)}, bf16[8,3,32,256]{3,2,1,0:T(8,128)(2,1)}, u32[]{:S(2)}, u32[]{:S(2)}) collective-permute-start(bf16[8,3,32,256]{3,2,1,0:T(8,128)(2,1)} %collective-permute-done.19.refs_12_), channel_id=1, source_target_pairs={{0,2},{2,4},{4,6},{6,0},{1,3},{3,5},{5,7},{7,1},{8,10},{10,12},{12... | collective-permute-start | bytes 1179656 | tf_op jit(solution)/shard_map/ppermute | solution.py:201
  78.2 17.3 %collective-permute-start.18 = (bf16[8,3,32,256]{3,2,1,0:T(8,128)(2,1)}, bf16[8,3,32,256]{3,2,1,0:T(8,128)(2,1)}, u32[]{:S(2)}, u32[]{:S(2)}) collective-permute-start(bf16[8,3,32,256]{3,2,1,0:T(8,128)(2,1)} %collective-permute-done.16.refs_9_), channel_id=1, source_target_pairs={{0,2},{2,4},{4,6},{6,0},{1,3},{3,5},{5,7},{7,1},{8,10},{10,12},{12... | collective-permute-start | bytes 1179656 | tf_op jit(solution)/shard_map/ppermute | solution.py:203
  78.8 2.2 %copy-start.17 = (bf16[3,8,32,256]{3,2,1,0:T(8,128)(2,1)}, bf16[3,8,32,256]{3,2,1,0:T(8,128)(2,1)S(1)}, u32[]{:S(2)}) copy-start(bf16[3,8,32,256]{3,2,1,0:T(8,128)(2,1)S(1)} %collective-permute-done.7.refs_7_) | copy-start | bytes 1179652
  78.8 16.8 %collective-permute-start.22 = (bf16[8,3,32,256]{3,2,1,0:T(8,128)(2,1)}, bf16[8,3,32,256]{3,2,1,0:T(8,128)(2,1)}, u32[]{:S(2)}, u32[]{:S(2)}) collective-permute-start(bf16[8,3,32,256]{3,2,1,0:T(8,128)(2,1)} %collective-permute-done.21.refs_14_), channel_id=1, source_target_pairs={{0,6},{2,0},{4,2},{6,4},{1,7},{3,1},{5,3},{7,5},{8,14},{10,8},{12,... | collective-permute-start | bytes 1179656 | tf_op jit(solution)/shard_map/ppermute | solution.py:203
  101.4 19.5 %all-to-all-start.2 = ((s16[64,8,512]{2,1,0:T(8,128)(2,1)}), s16[64,8,512]{2,1,0:T(8,128)(2,1)S(1)}, u32[]{:S(2)}, u32[]{:S(2)}) async-start(s16[64,8,512]{2,1,0:T(8,128)(2,1)} %bitcast.19), calls=%async_computation.2 | async-start | bytes 1048576 | tf_op jit(solution)/shard_map/all_to_all | solution.py:316
  110.0 35.3 %copy-start.6 = (s16[272,768]{1,0:T(8,128)(2,1)S(1)}, s16[272,768]{1,0:T(8,128)(2,1)}, u32[]{:S(2)}) copy-start(s16[272,768]{1,0:T(8,128)(2,1)} %get-tuple-element.16.refs_6_) | copy-start | bytes 1253380
  110.0 36.7 %copy-start.5 = (s16[272,768]{1,0:T(8,128)(2,1)S(1)}, s16[272,768]{1,0:T(8,128)(2,1)}, u32[]{:S(2)}) copy-start(s16[272,768]{1,0:T(8,128)(2,1)} %get-tuple-element.17.refs_5_) | copy-start | bytes 1253380
  110.0 35.3 %collective-permute-start.10 = (s16[272,768]{1,0:T(8,128)(2,1)}, s16[272,768]{1,0:T(8,128)(2,1)}, u32[]{:S(2)}, u32[]{:S(2)}) collective-permute-start(s16[272,768]{1,0:T(8,128)(2,1)} %get-tuple-element.18.refs_7_), channel_id=1, source_target_pairs={{0,14},{2,8},{4,10},{6,12},{8,6},{10,0},{12,2},{14,4},{1,15},{3,9}... | collective-permute-start | bytes 1253384 | tf_op jit(solution)/shard_map/ppermute | solution.py:298
  114.7 32.0 %collective-permute-start.11 = (s16[272,768]{1,0:T(8,128)(2,1)}, s16[272,768]{1,0:T(8,128)(2,1)}, u32[]{:S(2)}, u32[]{:S(2)}) collective-permute-start(s16[272,768]{1,0:T(8,128)(2,1)} %get-tuple-element.19.refs_2_), channel_id=1, source_target_pairs={{0,4},{2,6},{4,0},{6,2},{8,12},{10,14},{12,8},{14,10},{1,5},{3,7},... | collective-permute-start | bytes 1253384 | tf_op jit(solution)/shard_map/ppermute | solution.py:298
  121.0 0.8 copy-start.3
  124.2 66.7 %all-to-all-start.3 = ((s16[128,8,512]{2,1,0:T(8,128)(2,1)}), s16[128,8,512]{2,1,0:T(8,128)(2,1)S(1)}, u32[]{:S(2)}, u32[]{:S(2)}) async-start(s16[128,8,512]{2,1,0:T(8,128)(2,1)} %piece.1), calls=%async_computation.3 | async-start | bytes 2097152 | tf_op jit(solution)/shard_map/all_to_all | solution.py:324
  139.3 23.7 %collective-permute-start.12 = (s16[272,768]{1,0:T(8,128)(2,1)}, s16[272,768]{1,0:T(8,128)(2,1)S(1)}, u32[]{:S(2)}, u32[]{:S(2)}) collective-permute-start(s16[272,768]{1,0:T(8,128)(2,1)} %get-tuple-element.20.refs_4_), channel_id=1, source_target_pairs={{0,8},{2,10},{4,12},{6,14},{8,0},{10,2},{12,4},{14,6},{1,9},{3,11}... | collective-permute-start | bytes 1253384 | tf_op jit(solution)/shard_map/ppermute | solution.py:298
  142.6 20.4 %collective-permute-start.13 = (s16[272,768]{1,0:T(8,128)(2,1)}, s16[272,768]{1,0:T(8,128)(2,1)S(1)}, u32[]{:S(2)}, u32[]{:S(2)}) collective-permute-start(s16[272,768]{1,0:T(8,128)(2,1)} %get-tuple-element.21.refs_1_), channel_id=1, source_target_pairs={{0,2},{2,4},{4,6},{6,0},{8,10},{10,12},{12,14},{14,8},{1,3},{3,5},... | collective-permute-start | bytes 1253384 | tf_op jit(solution)/shard_map/ppermute | solution.py:298
  143.9 19.2 %collective-permute-start.14 = (s16[272,768]{1,0:T(8,128)(2,1)}, s16[272,768]{1,0:T(8,128)(2,1)S(1)}, u32[]{:S(2)}, u32[]{:S(2)}) collective-permute-start(s16[272,768]{1,0:T(8,128)(2,1)} %get-tuple-element.22.refs_3_), channel_id=1, source_target_pairs={{0,6},{2,0},{4,2},{6,4},{8,14},{10,8},{12,10},{14,12},{1,7},{3,1},... | collective-permute-start | bytes 1253384 | tf_op jit(solution)/shard_map/ppermute | solution.py:298
  145.3 29.0 %collective-permute-start.8 = (s16[272,768]{1,0:T(8,128)(2,1)S(1)}, s16[272,768]{1,0:T(8,128)(2,1)S(1)}, u32[]{:S(2)}, u32[]{:S(2)}) collective-permute-start(s16[272,768]{1,0:T(8,128)(2,1)S(1)} %copy-done.6), channel_id=1, source_target_pairs={{0,12},{2,14},{4,8},{6,10},{8,4},{10,6},{12,0},{14,2},{1,13},{3,15... | collective-permute-start | bytes 1253384 | tf_op jit(solution)/shard_map/ppermute | solution.py:298
  146.7 36.4 %collective-permute-start.9 = (s16[272,768]{1,0:T(8,128)(2,1)S(1)}, s16[272,768]{1,0:T(8,128)(2,1)}, u32[]{:S(2)}, u32[]{:S(2)}) collective-permute-start(s16[272,768]{1,0:T(8,128)(2,1)S(1)} %copy-done.5), channel_id=1, source_target_pairs={{0,10},{2,12},{4,14},{6,8},{8,2},{10,4},{12,6},{14,0},{1,11},{3,13... | collective-permute-start | bytes 1253384 | tf_op jit(solution)/shard_map/ppermute | solution.py:298
  163.1 11.3 %copy-start.7 = (s16[272,768]{1,0:T(8,128)(2,1)}, s16[272,768]{1,0:T(8,128)(2,1)S(1)}, u32[]{:S(2)}) copy-start(s16[272,768]{1,0:T(8,128)(2,1)S(1)} %collective-permute-done.12.refs_5_) | copy-start | bytes 1253380
  163.1 11.2 %copy-start.8 = (s16[272,768]{1,0:T(8,128)(2,1)}, s16[272,768]{1,0:T(8,128)(2,1)S(1)}, u32[]{:S(2)}) copy-start(s16[272,768]{1,0:T(8,128)(2,1)S(1)} %collective-permute-done.13.refs_6_) | copy-start | bytes 1253380
  163.1 11.2 %copy-start.9 = (s16[272,768]{1,0:T(8,128)(2,1)}, s16[272,768]{1,0:T(8,128)(2,1)S(1)}, u32[]{:S(2)}) copy-start(s16[272,768]{1,0:T(8,128)(2,1)S(1)} %collective-permute-done.14.refs_7_) | copy-start | bytes 1253380
  174.3 0.8 copy-start.10
  186.7 2.3 %collective-permute-start.15 = (bf16[128,768]{1,0:T(8,128)(2,1)}, bf16[128,768]{1,0:T(8,128)(2,1)S(1)}, u32[]{:S(2)}, u32[]{:S(2)}) collective-permute-start(bf16[128,768]{1,0:T(8,128)(2,1)} %get-tuple-element.24), channel_id=1, source_target_pairs={{0,1},{1,0},{2,3},{3,2},{4,5},{5,4},{6,7},{7,6},{8,9},{9,8},{10,11... | collective-permute-start | bytes 589832 | tf_op jit(solution)/shard_map/ppermute | solution.py:308
  190.8 1.0 copy-start.2
where the time goes:
time: 196 us; the launch traced here: 195 us
  waiting for transfers between devices  84.2 us (43%)
  starting transfers between devices  71.4 us (36%)
  Pallas kernels  30.3 us (15%)
  local copies, waits for them, and re-layouts  5.69 us (3%)
  other arithmetic  2.59 us (1%)
    ppermute x7, waiting for transfers between devices, update(): sums.append(lax.ppermute(coded[j], HY, to))  32.7 us
    all_to_all x1, waiting for transfers between devices, update(): lax.all_to_all(share, ('h', 'y', 'c'), split_axis=0, concat_axis=0, tiled...  21.6 us
    ppermute x7, starting transfers between devices, update(): sums.append(lax.ppermute(coded[j], HY, to))  15.7 us
    all_to_all x1, starting transfers between devices, update(): lax.all_to_all(piece, CHIPS + ('c',), split_axis=0, concat_axis=0, tiled=...  15.1 us
    pallas_call x1, Pallas kernels, update(): pl.pallas_call(product_kernel, out_shape=[jax.ShapeDtypeStruct((size + 16...  12.9 us
    all_to_all x1, starting transfers between devices, update(): lax.all_to_all(share, ('h', 'y', 'c'), split_axis=0, concat_axis=0, tiled...  9.35 us
    all_to_all x1, starting transfers between devices, update(): diag = lax.all_to_all(diag, CHIPS, split_axis=0, concat_axis=0, tiled=True)  8.57 us
    all_to_all x1, waiting for transfers between devices, update(): own = lax.all_to_all(own, XL, split_axis=0, concat_axis=0, tiled=True)  8.17 us
  transfers between devices with their start and end apart: 27, of which 13 were waited for; matrix products, arithmetic and copies ran while one was open for 2% of the time, Pallas kernels for 11%

commit v1 on v0

--- a/solution.py
+++ b/solution.py
@@ -246,6 +246,7 @@
         out_shape=[block, jax.ShapeDtypeStruct((groups, members, part, size), BF16)],
         in_specs=[smem, smem, vmem],
         out_specs=[vmem] * 2,
+        compiler_params=pltpu.CompilerParams(vmem_limit_bytes=8 << 20),
         name="pick",
     )(place, where, share)
     across = lax.ppermute(near, "l", CORE_SWAP)
@@ -273,6 +274,7 @@
                 pltpu.SemaphoreType.DMA((len(window_parts),)),
             ],
         ),
+        compiler_params=pltpu.CompilerParams(vmem_limit_bytes=20 << 20),
         name="product",
     )(place, where, ancestor_inv, other, *window_parts)
     pieces = groups * chips
@@ -284,6 +286,7 @@
         in_specs=[smem, smem] + [vmem] * (chips + len(row_parts)),
         out_specs=vmem,
         scratch_shapes=[pltpu.VMEM((size, width), F32)],
+        compiler_params=pltpu.CompilerParams(vmem_limit_bytes=16 << 20),
         name="diagonal",
     )(place, where, *coded, *row_parts)
 
@@ -302,6 +305,7 @@
         out_shape=[slab, slab],
         in_specs=[smem, smem] + [vmem] * len(sums),
         out_specs=[vmem] * 2,
+        compiler_params=pltpu.CompilerParams(vmem_limit_bytes=12 << 20),
         name="finish",
     )(place, where, *sums)
 
@@ -319,6 +323,7 @@
         out_shape=jax.ShapeDtypeStruct((pieces * NC, depth, reach), I16),
         in_specs=[vmem],
         out_specs=vmem,
+        compiler_params=pltpu.CompilerParams(vmem_limit_bytes=6 << 20),
         name="piece",
     )(diag)
     whole = lax.all_to_all(piece, CHIPS + ("c",), split_axis=0, concat_axis=0, tiled=True)
@@ -327,6 +332,7 @@
         out_shape=jax.ShapeDtypeStruct(diag_inverse.shape, F32),
         in_specs=[vmem, vmem],
         out_specs=vmem,
+        compiler_params=pltpu.CompilerParams(vmem_limit_bytes=12 << 20),
         name="total",
     )(whole.reshape(pieces, NC, depth, reach), diag_inverse)
     return column_block, diagonal

time: 196 us -> 188 us (0.959)
  Pallas kernels: 30.3 us -> 18.3 us
  local copies, waits for them, and re-layouts: 5.69 us -> 12.1 us
  waiting for transfers between devices: 84.2 us -> 82.1 us
    unnamed x40, local copies, waits for them, and re-layouts: 3.74 us -> 10.6 us
    pallas_call x1, Pallas kernels: 12.9 us -> 9.02 us  [update(): pl.pallas_call(product_kernel, out_shape=[jax.ShapeDtypeStruct((size + 16...]
    pallas_call x1, Pallas kernels: 5.87 us -> 3.65 us  [update(): pl.pallas_call(diagonal_kernel, out_shape=jax.ShapeDtypeStruct((2, size,...]
  transfers between devices with their start and end apart: 27 -> 27, of which waited for: 13 -> 10; matrix products, arithmetic and copies ran while one was open for 2% -> 1% of each run, Pallas kernels for 11% -> 7%
where the time goes in v1:
time: 188 us; the launch traced here: 187 us
  waiting for transfers between devices  82.1 us (44%)
  starting transfers between devices  73.1 us (39%)
  Pallas kernels  18.3 us (10%)
  local copies, waits for them, and re-layouts  12.1 us (6%)
    ppermute x7, waiting for transfers between devices, update(): sums.append(lax.ppermute(coded[j], HY, to))  33.4 us
    all_to_all x1, waiting for transfers between devices, update(): lax.all_to_all(share, ('h', 'y', 'c'), split_axis=0, concat_axis=0, tiled...  22.6 us
    all_to_all x1, starting transfers between devices, update(): lax.all_to_all(piece, CHIPS + ('c',), split_axis=0, concat_axis=0, tiled=...  15.8 us
    ppermute x7, starting transfers between devices, update(): sums.append(lax.ppermute(coded[j], HY, to))  15.6 us
    unnamed x40, local copies, waits for them, and re-layouts  10.6 us
    all_to_all x1, starting transfers between devices, update(): diag = lax.all_to_all(diag, CHIPS, split_axis=0, concat_axis=0, tiled=True)  9.41 us
    all_to_all x1, starting transfers between devices, update(): lax.all_to_all(share, ('h', 'y', 'c'), split_axis=0, concat_axis=0, tiled...  9.35 us
    pallas_call x1, Pallas kernels, update(): pl.pallas_call(product_kernel, out_shape=[jax.ShapeDtypeStruct((size + 16...  9.02 us
  transfers between devices with their start and end apart: 27, of which 10 were waited for; matrix products, arithmetic and copies ran while one was open for 1% of the time, Pallas kernels for 7%

profile of v1, /device:TPU:1, one launch (start us, length us, event | category | flops | bytes accessed | tf_op | source)
XLA Modules:
  0.0 187.5 jit_solution(15376046455955088705)
XLA Ops:
  0.6 1.5 collective-permute-start
  2.1 1.3 broadcast_in_dim.24
  3.5 9.4 %all-to-all-start = ((bf16[16,2,3,32,256]{4,3,2,1,0:T(8,128)(2,1)}), bf16[16,2,3,32,256]{4,3,2,1,0:T(8,128)(2,1)S(1)}, u32[]{:S(2)}, u32[]{:S(2)}) async-start(bf16[16,2,3,32,256]{4,3,2,1,0:T(8,128)(2,1)} %bitcast.18), calls=%async_computation | async-start | bytes 3145728 | tf_op jit(solution)/shard_map/all_to_all | solution.py:240
  13.1 22.6 %all-to-all-done = bf16[16,2,3,32,256]{4,3,2,1,0:T(8,128)(2,1)S(1)} async-done(((bf16[16,2,3,32,256]{4,3,2,1,0:T(8,128)(2,1)}), bf16[16,2,3,32,256]{4,3,2,1,0:T(8,128)(2,1)S(1)}, u32[]{:S(2)}, u32[]{:S(2)}) %all-to-all-start) | async-done | bytes 1572896 | tf_op jit(solution)/shard_map/all_to_all | solution.py:240
  35.7 0.8 pick.1
  37.3 0.7 collective-permute-start.4
  38.0 1.2 collective-permute-start.1
  39.2 4.2 %all-to-all-start.1 = ((bf16[8,3,32,256]{3,2,1,0:T(8,128)(2,1)}), bf16[8,3,32,256]{3,2,1,0:T(8,128)(2,1)S(1)}, u32[]{:S(2)}, u32[]{:S(2)}) async-start(bf16[8,3,32,256]{3,2,1,0:T(8,128)(2,1)} %copy-done.17), calls=%async_computation.1 | async-start | bytes 786432 | tf_op jit(solution)/shard_map/all_to_all | solution.py:255
  43.4 2.7 %collective-permute-start.2 = (bf16[3,8,32,256]{3,2,1,0:T(8,128)(2,1)S(1)}, bf16[3,8,32,256]{3,2,1,0:T(8,128)(2,1)S(1)}, u32[]{:S(2)}, u32[]{:S(2)}) collective-permute-start(bf16[3,8,32,256]{3,2,1,0:T(8,128)(2,1)S(1)} %get-tuple-element.14.refs_0_), channel_id=1, source_target_pairs={{0,96},{32,0},{64,32},{96,64},{1,97},{33,1},{65,33},{97,65},{2,98}... | collective-permute-start | bytes 1179656 | tf_op jit(solution)/shard_map/ppermute | solution.py:202
  46.1 8.0 %all-to-all-done.1.refs_8_ = bf16[8,3,32,256]{3,2,1,0:T(8,128)(2,1)S(1)} async-done(((bf16[8,3,32,256]{3,2,1,0:T(8,128)(2,1)}), bf16[8,3,32,256]{3,2,1,0:T(8,128)(2,1)S(1)}, u32[]{:S(2)}, u32[]{:S(2)}) %all-to-all-start.1) | async-done | bytes 393248 | tf_op jit(solution)/shard_map/all_to_all | solution.py:255
  54.0 1.2 collective-permute-start.19
  55.6 1.4 collective-permute-done.2.refs_2_
  56.9 0.7 copy-done.15
  57.7 1.4 collective-permute-start.5
  59.1 0.8 copy-done.11
  59.9 4.4 %collective-permute-done.19.refs_12_ = bf16[8,3,32,256]{3,2,1,0:T(8,128)(2,1)S(1)} collective-permute-done((bf16[8,3,32,256]{3,2,1,0:T(8,128)(2,1)S(1)}, bf16[8,3,32,256]{3,2,1,0:T(8,128)(2,1)S(1)}, u32[]{:S(2)}, u32[]{:S(2)}) %collective-permute-start.19) | collective-permute-done | bytes 393248 | tf_op jit(solution)/shard_map/ppermute | solution.py:256
  64.3 0.7 copy-done.13
  65.0 3.2 %collective-permute-start.21 = (bf16[8,3,32,256]{3,2,1,0:T(8,128)(2,1)S(1)}, bf16[8,3,32,256]{3,2,1,0:T(8,128)(2,1)S(1)}, u32[]{:S(2)}, u32[]{:S(2)}) collective-permute-start(bf16[8,3,32,256]{3,2,1,0:T(8,128)(2,1)S(1)} %collective-permute-done.19.refs_12_), channel_id=1, source_target_pairs={{0,6},{2,0},{4,2},{6,4},{1,7},{3,1},{5,3},{7,5},{8,14},{10,8},{12,... | collective-permute-start | bytes 1179656 | tf_op jit(solution)/shard_map/ppermute | solution.py:202
  68.2 2.7 %collective-permute-start.7 = (bf16[3,8,32,256]{3,2,1,0:T(8,128)(2,1)S(1)}, bf16[3,8,32,256]{3,2,1,0:T(8,128)(2,1)S(1)}, u32[]{:S(2)}, u32[]{:S(2)}) collective-permute-start(bf16[3,8,32,256]{3,2,1,0:T(8,128)(2,1)S(1)} %collective-permute-done.6.refs_6_), channel_id=1, source_target_pairs={{0,96},{32,0},{64,32},{96,64},{1,97},{33,1},{65,33},{97,65},{2,98}... | collective-permute-start | bytes 1179656 | tf_op jit(solution)/shard_map/ppermute | solution.py:203
  70.9 5.7 %collective-permute-done.3.refs_3_ = bf16[3,8,32,256]{3,2,1,0:T(8,128)(2,1)S(1)} collective-permute-done((bf16[3,8,32,256]{3,2,1,0:T(8,128)(2,1)S(1)}, bf16[3,8,32,256]{3,2,1,0:T(8,128)(2,1)S(1)}, u32[]{:S(2)}, u32[]{:S(2)}) %collective-permute-start.3) | collective-permute-done | bytes 393248 | tf_op jit(solution)/shard_map/ppermute | solution.py:203
  76.6 1.3 collective-permute-start.18
  77.9 1.4 collective-permute-start.22
  79.4 2.2 %copy-done.1 = bf16[2048,1024]{1,0:T(8,128)(2,1)S(1)} copy-done((bf16[2048,1024]{1,0:T(8,128)(2,1)S(1)}, bf16[2048,1024]{1,0:T(8,128)(2,1)}, u32[]{:S(2)}) %copy-start.1) | copy-done | bytes 4194328
  81.6 1.0 copy-done.10
  82.6 1.0 copy-done.12
  83.6 1.0 copy-done.14
  84.6 1.0 copy-done.16
  85.6 9.0 %product.1 = (s16[272,768]{1,0:T(8,128)(2,1)S(1)}, s16[272,768]{1,0:T(8,128)(2,1)S(1)}, s16[272,768]{1,0:T(8,128)(2,1)S(1)}, s16[272,768]{1,0:T(8,128)(2,1)S(1)}...) custom-call(s32[6,64]{1,0:T(8,128)S(1)} %select_reduce_fusion.place,, ...), custom_call_target="tpu_custom_call" | custom-call | tf_op jit(solution)/shard_map/product/pallas_call | solution.py:263
  94.7 3.7 %diagonal.1 = s16[2,256,512]{2,1,0:T(8,128)(2,1)} custom-call(s32[6,64]{1,0:T(8,128)S(1)} %select_reduce_fusion.place, s32[7]{0:T(128)S(1)} %stack.31.where, s16[272,768]{1,0:T(8,128)(2,1)S(1)} %get-tuple-element.15.refs_0_, s16[272,768]{1,0:T(8,128)(2,1)S(1)} %get-tuple-element.21.refs_1_, s16[272,768]{1,0:T(8,128)(2,1)S(1)} %get-tuple-element.19.refs_2_, ...), custom_call_target="tpu_custom_call" | custom-call | tf_op jit(solution)/shard_map/diagonal/pallas_call | solution.py:283
  98.4 9.4 %all-to-all-start.2 = ((s16[64,8,512]{2,1,0:T(8,128)(2,1)}), s16[64,8,512]{2,1,0:T(8,128)(2,1)S(1)}, u32[]{:S(2)}, u32[]{:S(2)}) async-start(s16[64,8,512]{2,1,0:T(8,128)(2,1)} %bitcast.12), calls=%async_computation.2 | async-start | bytes 1048576 | tf_op jit(solution)/shard_map/all_to_all | solution.py:320
  107.8 4.7 %collective-permute-start.10 = (s16[272,768]{1,0:T(8,128)(2,1)}, s16[272,768]{1,0:T(8,128)(2,1)}, u32[]{:S(2)}, u32[]{:S(2)}) collective-permute-start(s16[272,768]{1,0:T(8,128)(2,1)} %copy-done.8), channel_id=1, source_target_pairs={{0,14},{2,8},{4,10},{6,12},{8,6},{10,0},{12,2},{14,4},{1,15},{3,9}... | collective-permute-start | bytes 1253384 | tf_op jit(solution)/shard_map/ppermute | solution.py:301
  113.1 5.6 %all-to-all-done.2.q_ref = s16[64,8,512]{2,1,0:T(8,128)(2,1)S(1)} async-done(((s16[64,8,512]{2,1,0:T(8,128)(2,1)}), s16[64,8,512]{2,1,0:T(8,128)(2,1)S(1)}, u32[]{:S(2)}, u32[]{:S(2)}) %all-to-all-start.2) | async-done | bytes 524320 | tf_op jit(solution)/shard_map/all_to_all | solution.py:320
  118.7 1.3 piece.1
  120.1 15.8 %all-to-all-start.3 = ((s16[128,8,512]{2,1,0:T(8,128)(2,1)}), s16[128,8,512]{2,1,0:T(8,128)(2,1)S(1)}, u32[]{:S(2)}, u32[]{:S(2)}) async-start(s16[128,8,512]{2,1,0:T(8,128)(2,1)} %piece.1), calls=%async_computation.3 | async-start | bytes 2097152 | tf_op jit(solution)/shard_map/all_to_all | solution.py:329
  135.8 3.3 %collective-permute-start.12 = (s16[272,768]{1,0:T(8,128)(2,1)}, s16[272,768]{1,0:T(8,128)(2,1)S(1)}, u32[]{:S(2)}, u32[]{:S(2)}) collective-permute-start(s16[272,768]{1,0:T(8,128)(2,1)} %copy-done.6), channel_id=1, source_target_pairs={{0,8},{2,10},{4,12},{6,14},{8,0},{10,2},{12,4},{14,6},{1,9},{3,11}... | collective-permute-start | bytes 1253384 | tf_op jit(solution)/shard_map/ppermute | solution.py:301
  139.2 1.2 collective-permute-start.13
  140.4 1.4 collective-permute-start.14
  141.8 1.4 collective-permute-start.8
  143.3 3.0 %collective-permute-start.9 = (s16[272,768]{1,0:T(8,128)(2,1)S(1)}, s16[272,768]{1,0:T(8,128)(2,1)S(1)}, u32[]{:S(2)}, u32[]{:S(2)}) collective-permute-start(s16[272,768]{1,0:T(8,128)(2,1)S(1)} %get-tuple-element.17.refs_5_), channel_id=1, source_target_pairs={{0,10},{2,12},{4,14},{6,8},{8,2},{10,4},{12,6},{14,0},{1,11},{3,13... | collective-permute-start | bytes 1253384 | tf_op jit(solution)/shard_map/ppermute | solution.py:301
  146.2 13.4 %collective-permute-done.12.refs_5_ = s16[272,768]{1,0:T(8,128)(2,1)S(1)} collective-permute-done((s16[272,768]{1,0:T(8,128)(2,1)}, s16[272,768]{1,0:T(8,128)(2,1)S(1)}, u32[]{:S(2)}, u32[]{:S(2)}) %collective-permute-start.12) | collective-permute-done | bytes 417824 | tf_op jit(solution)/shard_map/ppermute | solution.py:301
  159.6 11.2 %collective-permute-done.8.refs_1_ = s16[272,768]{1,0:T(8,128)(2,1)S(1)} collective-permute-done((s16[272,768]{1,0:T(8,128)(2,1)}, s16[272,768]{1,0:T(8,128)(2,1)S(1)}, u32[]{:S(2)}, u32[]{:S(2)}) %collective-permute-start.8) | collective-permute-done | bytes 417824 | tf_op jit(solution)/shard_map/ppermute | solution.py:301
  170.8 8.8 %collective-permute-done.9.refs_2_ = s16[272,768]{1,0:T(8,128)(2,1)S(1)} collective-permute-done((s16[272,768]{1,0:T(8,128)(2,1)S(1)}, s16[272,768]{1,0:T(8,128)(2,1)S(1)}, u32[]{:S(2)}, u32[]{:S(2)}) %collective-permute-start.9) | collective-permute-done | bytes 417824 | tf_op jit(solution)/shard_map/ppermute | solution.py:301
  179.6 2.0 %finish.1 = (bf16[128,768]{1,0:T(8,128)(2,1)S(1)}, bf16[128,768]{1,0:T(8,128)(2,1)S(1)}) custom-call(s32[6,64]{1,0:T(8,128)S(1)} %select_reduce_fusion.place, s32[7]{0:T(128)S(1)} %stack.31.where, s16[272,768]{1,0:T(8,128)(2,1)S(1)} %get-tuple-element.15.refs_0_, s16[272,768]{1,0:T(8,128)(2,1)S(1)} %collective-permute-done.8.refs_1_, ...), custom_call_target="tpu_custom_call" | custom-call | tf_op jit(solution)/shard_map/finish/pallas_call | solution.py:303
  181.6 1.1 collective-permute-start.15
  182.7 1.1 collective-permute-done.15
  183.8 0.8 maximum_select_fusion
  184.6 1.4 copy-done.2
  186.0 1.5 total.1
  (59 shorter events, 2.1 us)
Async XLA Ops:
  0.6 1.5 copy-start
  0.6 78.7 %collective-permute-start = (bf16[2048,1024]{1,0:T(8,128)(2,1)}, bf16[2048,1024]{1,0:T(8,128)(2,1)}, u32[]{:S(2)}, u32[]{:S(2)}) collective-permute-start(bf16[2048,1024]{1,0:T(8,128)(2,1)} %own_ref.1), channel_id=1, source_target_pairs={{0,1},{1,0},{2,3},{3,2},{4,5},{5,4},{6,7},{7,6},{8,9},{9,8},{10,11... | collective-permute-start | bytes 12582920 | tf_op jit(solution)/shard_map/ppermute | solution.py:227
  3.5 9.4 %copy-start.18 = (s32[6,32]{1,0:T(8,128)S(1)}, s32[6,32]{1,0:T(8,128)}, u32[]{:S(2)}) copy-start(s32[6,32]{1,0:T(8,128)} %param.8) | copy-start | bytes 2308
  3.5 9.5 %copy-start.19 = (s32[6,32]{1,0:T(8,128)S(1)}, s32[6,32]{1,0:T(8,128)}, u32[]{:S(2)}) copy-start(s32[6,32]{1,0:T(8,128)} %param.7) | copy-start | bytes 2308
  3.5 32.2 %all-to-all-start = ((bf16[16,2,3,32,256]{4,3,2,1,0:T(8,128)(2,1)}), bf16[16,2,3,32,256]{4,3,2,1,0:T(8,128)(2,1)S(1)}, u32[]{:S(2)}, u32[]{:S(2)}) async-start(bf16[16,2,3,32,256]{4,3,2,1,0:T(8,128)(2,1)} %bitcast.18), calls=%async_computation | async-start | bytes 3145728 | tf_op jit(solution)/shard_map/all_to_all | solution.py:240
  36.5 0.7 copy-start.17
  37.3 42.1 %copy-start.9 = (bf16[3,8,32,256]{3,2,1,0:T(8,128)(2,1)}, bf16[3,8,32,256]{3,2,1,0:T(8,128)(2,1)S(1)}, u32[]{:S(2)}) copy-start(bf16[3,8,32,256]{3,2,1,0:T(8,128)(2,1)S(1)} %get-tuple-element.14.refs_0_) | copy-start | bytes 1179652
  37.3 17.9 %collective-permute-start.4 = (bf16[3,8,32,256]{3,2,1,0:T(8,128)(2,1)S(1)}, bf16[3,8,32,256]{3,2,1,0:T(8,128)(2,1)S(1)}, u32[]{:S(2)}, u32[]{:S(2)}) collective-permute-start(bf16[3,8,32,256]{3,2,1,0:T(8,128)(2,1)S(1)} %get-tuple-element.14.refs_0_), channel_id=1, source_target_pairs={{0,16},{16,0},{1,17},{17,1},{2,18},{18,2},{3,19},{19,3},{4,20},{20... | collective-permute-start | bytes 1179656 | tf_op jit(solution)/shard_map/ppermute | solution.py:252
  38.0 17.6 %collective-permute-start.1 = (bf16[3,8,32,256]{3,2,1,0:T(8,128)(2,1)S(1)}, bf16[3,8,32,256]{3,2,1,0:T(8,128)(2,1)S(1)}, u32[]{:S(2)}, u32[]{:S(2)}) collective-permute-start(bf16[3,8,32,256]{3,2,1,0:T(8,128)(2,1)S(1)} %get-tuple-element.14.refs_0_), channel_id=1, source_target_pairs={{0,32},{32,64},{64,96},{96,0},{1,33},{33,65},{65,97},{97,1},{2,34}... | collective-permute-start | bytes 1179656 | tf_op jit(solution)/shard_map/ppermute | solution.py:201
  39.2 14.8 %all-to-all-start.1 = ((bf16[8,3,32,256]{3,2,1,0:T(8,128)(2,1)}), bf16[8,3,32,256]{3,2,1,0:T(8,128)(2,1)S(1)}, u32[]{:S(2)}, u32[]{:S(2)}) async-start(bf16[8,3,32,256]{3,2,1,0:T(8,128)(2,1)} %copy-done.17), calls=%async_computation.1 | async-start | bytes 786432 | tf_op jit(solution)/shard_map/all_to_all | solution.py:255
  43.4 13.5 %collective-permute-start.2 = (bf16[3,8,32,256]{3,2,1,0:T(8,128)(2,1)S(1)}, bf16[3,8,32,256]{3,2,1,0:T(8,128)(2,1)S(1)}, u32[]{:S(2)}, u32[]{:S(2)}) collective-permute-start(bf16[3,8,32,256]{3,2,1,0:T(8,128)(2,1)S(1)} %get-tuple-element.14.refs_0_), channel_id=1, source_target_pairs={{0,96},{32,0},{64,32},{96,64},{1,97},{33,1},{65,33},{97,65},{2,98}... | collective-permute-start | bytes 1179656 | tf_op jit(solution)/shard_map/ppermute | solution.py:202
  54.0 10.3 %collective-permute-start.19 = (bf16[8,3,32,256]{3,2,1,0:T(8,128)(2,1)S(1)}, bf16[8,3,32,256]{3,2,1,0:T(8,128)(2,1)S(1)}, u32[]{:S(2)}, u32[]{:S(2)}) collective-permute-start(bf16[8,3,32,256]{3,2,1,0:T(8,128)(2,1)S(1)} %all-to-all-done.1.refs_8_), channel_id=1, source_target_pairs={{0,8},{8,0},{1,9},{9,1},{2,10},{10,2},{3,11},{11,3},{4,12},{12,4},... | collective-permute-start | bytes 1179656 | tf_op jit(solution)/shard_map/ppermute | solution.py:256
  55.2 9.8 %collective-permute-start.16 = (bf16[8,3,32,256]{3,2,1,0:T(8,128)(2,1)S(1)}, bf16[8,3,32,256]{3,2,1,0:T(8,128)(2,1)S(1)}, u32[]{:S(2)}, u32[]{:S(2)}) collective-permute-start(bf16[8,3,32,256]{3,2,1,0:T(8,128)(2,1)S(1)} %all-to-all-done.1.refs_8_), channel_id=1, source_target_pairs={{0,2},{2,4},{4,6},{6,0},{1,3},{3,5},{5,7},{7,1},{8,10},{10,12},{12... | collective-permute-start | bytes 1179656 | tf_op jit(solution)/shard_map/ppermute | solution.py:201
  55.6 12.6 %collective-permute-start.6 = (bf16[3,8,32,256]{3,2,1,0:T(8,128)(2,1)S(1)}, bf16[3,8,32,256]{3,2,1,0:T(8,128)(2,1)S(1)}, u32[]{:S(2)}, u32[]{:S(2)}) collective-permute-start(bf16[3,8,32,256]{3,2,1,0:T(8,128)(2,1)S(1)} %collective-permute-done.4.refs_4_), channel_id=1, source_target_pairs={{0,96},{32,0},{64,32},{96,64},{1,97},{33,1},{65,33},{97,65},{2,98}... | collective-permute-start | bytes 1179656 | tf_op jit(solution)/shard_map/ppermute | solution.py:202
  56.9 0.7 copy-start.15
  57.7 13.2 %collective-permute-start.5 = (bf16[3,8,32,256]{3,2,1,0:T(8,128)(2,1)S(1)}, bf16[3,8,32,256]{3,2,1,0:T(8,128)(2,1)S(1)}, u32[]{:S(2)}, u32[]{:S(2)}) collective-permute-start(bf16[3,8,32,256]{3,2,1,0:T(8,128)(2,1)S(1)} %collective-permute-done.4.refs_4_), channel_id=1, source_target_pairs={{0,32},{32,64},{64,96},{96,0},{1,33},{33,65},{65,97},{97,1},{2,34}... | collective-permute-start | bytes 1179656 | tf_op jit(solution)/shard_map/ppermute | solution.py:201
  59.1 0.8 copy-start.11
  64.3 12.3 %collective-permute-start.3 = (bf16[3,8,32,256]{3,2,1,0:T(8,128)(2,1)S(1)}, bf16[3,8,32,256]{3,2,1,0:T(8,128)(2,1)S(1)}, u32[]{:S(2)}, u32[]{:S(2)}) collective-permute-start(bf16[3,8,32,256]{3,2,1,0:T(8,128)(2,1)S(1)} %collective-permute-done.1.refs_1_), channel_id=1, source_target_pairs={{0,32},{32,64},{64,96},{96,0},{1,33},{33,65},{65,97},{97,1},{2,34}... | collective-permute-start | bytes 1179656 | tf_op jit(solution)/shard_map/ppermute | solution.py:203
  64.3 0.7 copy-start.13
  65.0 11.6 %collective-permute-start.21 = (bf16[8,3,32,256]{3,2,1,0:T(8,128)(2,1)S(1)}, bf16[8,3,32,256]{3,2,1,0:T(8,128)(2,1)S(1)}, u32[]{:S(2)}, u32[]{:S(2)}) collective-permute-start(bf16[8,3,32,256]{3,2,1,0:T(8,128)(2,1)S(1)} %collective-permute-done.19.refs_12_), channel_id=1, source_target_pairs={{0,6},{2,0},{4,2},{6,4},{1,7},{3,1},{5,3},{7,5},{8,14},{10,8},{12,... | collective-permute-start | bytes 1179656 | tf_op jit(solution)/shard_map/ppermute | solution.py:202
  68.2 9.8 %collective-permute-start.7 = (bf16[3,8,32,256]{3,2,1,0:T(8,128)(2,1)S(1)}, bf16[3,8,32,256]{3,2,1,0:T(8,128)(2,1)S(1)}, u32[]{:S(2)}, u32[]{:S(2)}) collective-permute-start(bf16[3,8,32,256]{3,2,1,0:T(8,128)(2,1)S(1)} %collective-permute-done.6.refs_6_), channel_id=1, source_target_pairs={{0,96},{32,0},{64,32},{96,64},{1,97},{33,1},{65,33},{97,65},{2,98}... | collective-permute-start | bytes 1179656 | tf_op jit(solution)/shard_map/ppermute | solution.py:203
  70.9 23.8 %collective-permute-start.17 = (bf16[8,3,32,256]{3,2,1,0:T(8,128)(2,1)S(1)}, bf16[8,3,32,256]{3,2,1,0:T(8,128)(2,1)S(1)}, u32[]{:S(2)}, u32[]{:S(2)}) collective-permute-start(bf16[8,3,32,256]{3,2,1,0:T(8,128)(2,1)S(1)} %all-to-all-done.1.refs_8_), channel_id=1, source_target_pairs={{0,6},{2,0},{4,2},{6,4},{1,7},{3,1},{5,3},{7,5},{8,14},{10,8},{12,... | collective-permute-start | bytes 1179656 | tf_op jit(solution)/shard_map/ppermute | solution.py:202
  76.6 18.0 %collective-permute-start.20 = (bf16[8,3,32,256]{3,2,1,0:T(8,128)(2,1)S(1)}, bf16[8,3,32,256]{3,2,1,0:T(8,128)(2,1)S(1)}, u32[]{:S(2)}, u32[]{:S(2)}) collective-permute-start(bf16[8,3,32,256]{3,2,1,0:T(8,128)(2,1)S(1)} %collective-permute-done.19.refs_12_), channel_id=1, source_target_pairs={{0,2},{2,4},{4,6},{6,0},{1,3},{3,5},{5,7},{7,1},{8,10},{10,12},{12... | collective-permute-start | bytes 1179656 | tf_op jit(solution)/shard_map/ppermute | solution.py:201
  76.6 18.0 %collective-permute-start.18 = (bf16[8,3,32,256]{3,2,1,0:T(8,128)(2,1)S(1)}, bf16[8,3,32,256]{3,2,1,0:T(8,128)(2,1)S(1)}, u32[]{:S(2)}, u32[]{:S(2)}) collective-permute-start(bf16[8,3,32,256]{3,2,1,0:T(8,128)(2,1)S(1)} %collective-permute-done.16.refs_9_), channel_id=1, source_target_pairs={{0,2},{2,4},{4,6},{6,0},{1,3},{3,5},{5,7},{7,1},{8,10},{10,12},{12... | collective-permute-start | bytes 1179656 | tf_op jit(solution)/shard_map/ppermute | solution.py:203
  77.9 16.7 %collective-permute-start.22 = (bf16[8,3,32,256]{3,2,1,0:T(8,128)(2,1)S(1)}, bf16[8,3,32,256]{3,2,1,0:T(8,128)(2,1)S(1)}, u32[]{:S(2)}, u32[]{:S(2)}) collective-permute-start(bf16[8,3,32,256]{3,2,1,0:T(8,128)(2,1)S(1)} %collective-permute-done.21.refs_14_), channel_id=1, source_target_pairs={{0,6},{2,0},{4,2},{6,4},{1,7},{3,1},{5,3},{7,5},{8,14},{10,8},{12,... | collective-permute-start | bytes 1179656 | tf_op jit(solution)/shard_map/ppermute | solution.py:203
  79.4 2.2 %copy-start.1 = (bf16[2048,1024]{1,0:T(8,128)(2,1)S(1)}, bf16[2048,1024]{1,0:T(8,128)(2,1)}, u32[]{:S(2)}) copy-start(bf16[2048,1024]{1,0:T(8,128)(2,1)} %own_ref.1) | copy-start | bytes 12582916
  81.6 1.0 copy-start.10
  82.6 1.0 copy-start.12
  83.6 1.0 copy-start.14
  84.6 1.0 copy-start.16
  94.6 3.8 %copy-start.3 = (s16[272,768]{1,0:T(8,128)(2,1)}, s16[272,768]{1,0:T(8,128)(2,1)S(1)}, u32[]{:S(2)}) copy-start(s16[272,768]{1,0:T(8,128)(2,1)S(1)} %get-tuple-element.16.refs_6_) | copy-start | bytes 1253380
  94.6 3.8 %copy-start.4 = (s16[272,768]{1,0:T(8,128)(2,1)}, s16[272,768]{1,0:T(8,128)(2,1)S(1)}, u32[]{:S(2)}) copy-start(s16[272,768]{1,0:T(8,128)(2,1)S(1)} %get-tuple-element.22.refs_3_) | copy-start | bytes 1253380
  94.6 3.7 %copy-start.5 = (s16[272,768]{1,0:T(8,128)(2,1)}, s16[272,768]{1,0:T(8,128)(2,1)S(1)}, u32[]{:S(2)}) copy-start(s16[272,768]{1,0:T(8,128)(2,1)S(1)} %get-tuple-element.21.refs_1_) | copy-start | bytes 1253380
  94.6 3.7 %copy-start.7 = (s16[272,768]{1,0:T(8,128)(2,1)}, s16[272,768]{1,0:T(8,128)(2,1)S(1)}, u32[]{:S(2)}) copy-start(s16[272,768]{1,0:T(8,128)(2,1)S(1)} %get-tuple-element.19.refs_2_) | copy-start | bytes 1253380
  94.6 3.7 %copy-start.8 = (s16[272,768]{1,0:T(8,128)(2,1)}, s16[272,768]{1,0:T(8,128)(2,1)S(1)}, u32[]{:S(2)}) copy-start(s16[272,768]{1,0:T(8,128)(2,1)S(1)} %get-tuple-element.18.refs_7_) | copy-start | bytes 1253380
  94.6 3.7 %copy-start.6 = (s16[272,768]{1,0:T(8,128)(2,1)}, s16[272,768]{1,0:T(8,128)(2,1)S(1)}, u32[]{:S(2)}) copy-start(s16[272,768]{1,0:T(8,128)(2,1)S(1)} %get-tuple-element.20.refs_4_) | copy-start | bytes 1253380
  98.4 20.3 %all-to-all-start.2 = ((s16[64,8,512]{2,1,0:T(8,128)(2,1)}), s16[64,8,512]{2,1,0:T(8,128)(2,1)S(1)}, u32[]{:S(2)}, u32[]{:S(2)}) async-start(s16[64,8,512]{2,1,0:T(8,128)(2,1)} %bitcast.12), calls=%async_computation.2 | async-start | bytes 1048576 | tf_op jit(solution)/shard_map/all_to_all | solution.py:320
  107.8 34.0 %collective-permute-start.10 = (s16[272,768]{1,0:T(8,128)(2,1)}, s16[272,768]{1,0:T(8,128)(2,1)}, u32[]{:S(2)}, u32[]{:S(2)}) collective-permute-start(s16[272,768]{1,0:T(8,128)(2,1)} %copy-done.8), channel_id=1, source_target_pairs={{0,14},{2,8},{4,10},{6,12},{8,6},{10,0},{12,2},{14,4},{1,15},{3,9}... | collective-permute-start | bytes 1253384 | tf_op jit(solution)/shard_map/ppermute | solution.py:301
  112.5 30.7 %collective-permute-start.11 = (s16[272,768]{1,0:T(8,128)(2,1)}, s16[272,768]{1,0:T(8,128)(2,1)}, u32[]{:S(2)}, u32[]{:S(2)}) collective-permute-start(s16[272,768]{1,0:T(8,128)(2,1)} %copy-done.7), channel_id=1, source_target_pairs={{0,4},{2,6},{4,0},{6,2},{8,12},{10,14},{12,8},{14,10},{1,5},{3,7},... | collective-permute-start | bytes 1253384 | tf_op jit(solution)/shard_map/ppermute | solution.py:301
  120.1 64.5 %all-to-all-start.3 = ((s16[128,8,512]{2,1,0:T(8,128)(2,1)}), s16[128,8,512]{2,1,0:T(8,128)(2,1)S(1)}, u32[]{:S(2)}, u32[]{:S(2)}) async-start(s16[128,8,512]{2,1,0:T(8,128)(2,1)} %piece.1), calls=%async_computation.3 | async-start | bytes 2097152 | tf_op jit(solution)/shard_map/all_to_all | solution.py:329
  135.8 23.7 %collective-permute-start.12 = (s16[272,768]{1,0:T(8,128)(2,1)}, s16[272,768]{1,0:T(8,128)(2,1)S(1)}, u32[]{:S(2)}, u32[]{:S(2)}) collective-permute-start(s16[272,768]{1,0:T(8,128)(2,1)} %copy-done.6), channel_id=1, source_target_pairs={{0,8},{2,10},{4,12},{6,14},{8,0},{10,2},{12,4},{14,6},{1,9},{3,11}... | collective-permute-start | bytes 1253384 | tf_op jit(solution)/shard_map/ppermute | solution.py:301
  139.2 20.4 %collective-permute-start.13 = (s16[272,768]{1,0:T(8,128)(2,1)}, s16[272,768]{1,0:T(8,128)(2,1)S(1)}, u32[]{:S(2)}, u32[]{:S(2)}) collective-permute-start(s16[272,768]{1,0:T(8,128)(2,1)} %copy-done.5), channel_id=1, source_target_pairs={{0,2},{2,4},{4,6},{6,0},{8,10},{10,12},{12,14},{14,8},{1,3},{3,5},... | collective-permute-start | bytes 1253384 | tf_op jit(solution)/shard_map/ppermute | solution.py:301
  140.4 19.2 %collective-permute-start.14 = (s16[272,768]{1,0:T(8,128)(2,1)}, s16[272,768]{1,0:T(8,128)(2,1)S(1)}, u32[]{:S(2)}, u32[]{:S(2)}) collective-permute-start(s16[272,768]{1,0:T(8,128)(2,1)} %copy-done.4), channel_id=1, source_target_pairs={{0,6},{2,0},{4,2},{6,4},{8,14},{10,8},{12,10},{14,12},{1,7},{3,1},... | collective-permute-start | bytes 1253384 | tf_op jit(solution)/shard_map/ppermute | solution.py:301
  141.8 29.0 %collective-permute-start.8 = (s16[272,768]{1,0:T(8,128)(2,1)}, s16[272,768]{1,0:T(8,128)(2,1)S(1)}, u32[]{:S(2)}, u32[]{:S(2)}) collective-permute-start(s16[272,768]{1,0:T(8,128)(2,1)} %copy-done.3), channel_id=1, source_target_pairs={{0,12},{2,14},{4,8},{6,10},{8,4},{10,6},{12,0},{14,2},{1,13},{3,15... | collective-permute-start | bytes 1253384 | tf_op jit(solution)/shard_map/ppermute | solution.py:301
  143.3 36.3 %collective-permute-start.9 = (s16[272,768]{1,0:T(8,128)(2,1)S(1)}, s16[272,768]{1,0:T(8,128)(2,1)S(1)}, u32[]{:S(2)}, u32[]{:S(2)}) collective-permute-start(s16[272,768]{1,0:T(8,128)(2,1)S(1)} %get-tuple-element.17.refs_5_), channel_id=1, source_target_pairs={{0,10},{2,12},{4,14},{6,8},{8,2},{10,4},{12,6},{14,0},{1,11},{3,13... | collective-permute-start | bytes 1253384 | tf_op jit(solution)/shard_map/ppermute | solution.py:301
  181.6 2.1 %collective-permute-start.15 = (bf16[128,768]{1,0:T(8,128)(2,1)S(1)}, bf16[128,768]{1,0:T(8,128)(2,1)S(1)}, u32[]{:S(2)}, u32[]{:S(2)}) collective-permute-start(bf16[128,768]{1,0:T(8,128)(2,1)S(1)} %get-tuple-element.24), channel_id=1, source_target_pairs={{0,1},{1,0},{2,3},{3,2},{4,5},{5,4},{6,7},{7,6},{8,9},{9,8},{10,11... | collective-permute-start | bytes 589832 | tf_op jit(solution)/shard_map/ppermute | solution.py:312
  184.6 1.4 copy-start.2
